TPU v7x, 32 devices: a whole 2x2x4 slice. The times are simulated.
32 devices in a mesh: node: 4 (over z), dom: 8 (over y, x, core).
Axes of the slice: x: 2, y: 2, z: 4, core: 2. Of those that a mesh axis runs over, the one named last changes fastest.
Arguments:
- probes: float32 [32, 16, 16, 128], P(None, 'dom'), may hold values from -24 to 24
- slope: float32 [16, 16, 128], P('dom'), may hold values from 4 to 6
- root: float32 [16, 16, 128], P('dom'), may hold values from 0.3 to 0.7
- damping: float32 [16, 16, 128], P('dom'), may hold values from 0.3 to 1.2
Outputs:
- moments: float32 [2, 2, 32, 16, 16, 128], P(None, None, 'node', 'dom')
- projections: float32 [2, 2, 32, 32], replicated
All inputs are finite; a program needn't handle non-finite values.
Results may differ from a plain program's by a relative error of at most 0.00013.
Values sent between devices are 32-bit elements; how exact they have to be, the bound alone decides.
A program may use at most 64 MiB of HBM per device.

v0:
```python
import math
import jax
import jax.numpy as jnp
from jax import lax
from jax.sharding import PartitionSpec as P

NODE_DEV = 2
SWEEPS = 8
CENTRE = 0.5
RADIUS = 2.0


def grid_step(source, fields, factor_re, factor_im):
    padded = jnp.pad(fields, ((0, 0), (0, 0), (1, 1), (1, 1), (1, 1)))
    total = padded[:, :, 2:, 1:-1, 1:-1] + padded[:, :, :-2, 1:-1, 1:-1]
    total = total + padded[:, :, 1:-1, 2:, 1:-1] + padded[:, :, 1:-1, :-2, 1:-1]
    total = total + padded[:, :, 1:-1, 1:-1, 2:] + padded[:, :, 1:-1, 1:-1, :-2]
    real_part = source + total[:, 0]
    imag_part = total[:, 1]
    return jnp.stack(
        [
            real_part * factor_re - imag_part * factor_im,
            real_part * factor_im + imag_part * factor_re,
        ],
        axis=1,
    )


def inverse_diagonal(shift_real, shift_imaginary, slope, root, damping, guard):
    zr_col = shift_real[:, None, None, None, None]
    zi_col = shift_imaginary[:, None, None, None, None]
    decay = jnp.exp(-zr_col)
    real_d = slope * (zr_col - root) + damping * (decay * jnp.cos(zi_col))
    imag_d = slope * zi_col - damping * (decay * jnp.sin(zi_col))
    scale = 1.0 / (real_d * real_d + imag_d * imag_d + guard)
    return (real_d * scale, -imag_d * scale)


def per_system(fields, weight_re, weight_im):
    a_col = weight_re[:, None, None, None]
    b_col = weight_im[:, None, None, None]
    return jnp.stack(
        [a_col * fields[:, 0] - b_col * fields[:, 1], a_col * fields[:, 1] + b_col * fields[:, 0]]
    )


def body(probes, slope, root, damping):
    vectors = probes.shape[0]
    planes = probes.shape[1]
    groups = lax.axis_size("node")
    total = NODE_DEV * groups
    first = (lax.axis_index("node") * NODE_DEV).astype(jnp.float32)
    dom_size = lax.axis_size("dom")
    count = NODE_DEV * vectors // dom_size
    replicated = jnp.broadcast_to(probes[None], (NODE_DEV,) + probes.shape).reshape(
        (NODE_DEV * vectors,) + probes.shape[1:]
    )
    own = lax.all_to_all(replicated, "dom", split_axis=0, concat_axis=1, tiled=True)
    slope_all, root_all, damping_all = (
        lax.all_gather(slope, "dom", axis=0, tiled=True),
        lax.all_gather(root, "dom", axis=0, tiled=True),
        lax.all_gather(damping, "dom", axis=0, tiled=True),
    )
    system = lax.axis_index("dom") * count + jnp.arange(count)
    position = first + (system // vectors).astype(jnp.float32)
    theta = 2.0 * math.pi * (position + 0.5) / total
    shift_real = CENTRE + RADIUS * jnp.cos(theta)
    shift_imaginary = RADIUS * jnp.sin(theta)
    qre, qim = inverse_diagonal(
        shift_real, shift_imaginary, slope_all[None], root_all[None], damping_all[None], 0.0
    )
    qre = qre[:, 0]
    qim = qim[:, 0]
    fields = jnp.stack([own * qre, own * qim], axis=1)
    for sweep in range(SWEEPS):
        fields = grid_step(own, fields, qre, qim)
    weight_re = RADIUS * jnp.cos(theta) / total
    weight_im = RADIUS * jnp.sin(theta) / total
    shifted_re = weight_re * shift_real - weight_im * shift_imaginary
    shifted_im = weight_re * shift_imaginary + weight_im * shift_real
    terms = jnp.stack(
        [per_system(fields, weight_re, weight_im), per_system(fields, shifted_re, shifted_im)]
    )
    back = lax.all_to_all(terms, "dom", split_axis=3, concat_axis=2, tiled=True)
    local = jnp.sum(back.reshape((2, 2, NODE_DEV, vectors) + probes.shape[1:]), axis=2)
    flat = local.reshape(4 * vectors, -1)
    basis = probes.reshape(vectors, -1)
    partial_value = lax.dot_general(
        flat,
        basis,
        (((1,), (1,)), ((), ())),
        precision=lax.Precision.HIGHEST,
        preferred_element_type=jnp.float32,
    )
    cells = planes * probes.shape[2] * probes.shape[3] * lax.axis_size("dom")
    projections = lax.psum(partial_value.reshape(2, 2, vectors, vectors) / cells, ("node", "dom"))
    summed = lax.psum(local, "node")
    share = vectors // groups
    moments = lax.dynamic_slice_in_dim(summed, lax.axis_index("node") * share, share, 2)
    return (moments, projections)


def solution(mesh):
    in_specs = (
        P(None, "dom", None, None),
        P("dom", None, None),
        P("dom", None, None),
        P("dom", None, None),
    )
    out_specs = (P(None, None, "node", "dom", None, None), P())
    return jax.shard_map(body, mesh=mesh, in_specs=in_specs, out_specs=out_specs, check_vma=False)
```

profile of v0, /device:TPU:0, one launch (start us, length us, event | category | flops | bytes accessed | tf_op | source)
XLA Modules:
  0.0 260.8 jit_solution(6893673430703613702)
XLA Ops:
  7.2 0.0 copy-start.2
  7.2 0.0 copy-start.3
  7.2 0.0 copy-start.4
  7.2 2.2 broadcast_in_dim.2
  9.4 5.2 %all-to-all-start = ((f32[64,2,16,128]{3,2,1,0:T(8,128)}), f32[64,2,16,128]{3,2,1,0:T(8,128)S(1)}, u32[]{:S(2)}, u32[]{:S(2)}) async-start(f32[64,2,16,128]{3,2,1,0:T(8,128)} %bitcast), calls=%async_computation | async-start | bytes 2097152 | tf_op jit(solution)/shard_map/all_to_all | solution.py:58
  14.6 0.0 copy-done.2
  14.6 18.8 %all_gather.9 = f32[16,16,128]{2,1,0:T(8,128)S(1)} all-gather(f32[2,16,128]{2,1,0:T(8,128)S(1)} %copy-done.2), channel_id=1, replica_groups=mesh['node'=4,'dom'=8] {'dom'}, dimensions={0}, use_global_device_ids=true | all-gather | bytes 147456 | tf_op jit(solution)/shard_map/all_gather | solution.py:60
  33.4 0.0 copy-done.3
  33.4 8.3 %all_gather.10 = f32[16,16,128]{2,1,0:T(8,128)S(1)} all-gather(f32[2,16,128]{2,1,0:T(8,128)S(1)} %copy-done.3), channel_id=1, replica_groups=mesh['node'=4,'dom'=8] {'dom'}, dimensions={0}, use_global_device_ids=true | all-gather | bytes 147456 | tf_op jit(solution)/shard_map/all_gather | solution.py:61
  41.7 0.0 copy-done.4
  41.7 9.1 %all_gather.11 = f32[16,16,128]{2,1,0:T(8,128)S(1)} all-gather(f32[2,16,128]{2,1,0:T(8,128)S(1)} %copy-done.4), channel_id=1, replica_groups=mesh['node'=4,'dom'=8] {'dom'}, dimensions={0}, use_global_device_ids=true | all-gather | bytes 147456 | tf_op jit(solution)/shard_map/all_gather | solution.py:62
  50.8 0.1 multiply_subtract_fusion.12
  50.9 0.0 all-to-all-done
  50.9 0.1 copy.15
  51.0 0.6 fusion.19
  51.6 2.6 select_maximum_fusion.7
  54.2 3.3 %slice_add_fusion.35 = f32[8,2,16,16,128]{4,3,2,0,1:T(8,128)S(1)} fusion(f32[8,2,18,18,130]{4,3,2,0,1:T(8,128)S(1)} %select_maximum_fusion.7), kind=kLoop, calls=%fused_computation.56 | loop fusion | flops 2621440 | bytes 14680064 | tf_op jit(solution)/shard_map/add | solution.py:17
  57.5 0.8 multiply_subtract_fusion.10
  58.3 2.4 select_maximum_fusion.6
  60.7 3.3 %slice_add_fusion.30 = f32[8,2,16,16,128]{4,3,2,0,1:T(8,128)S(1)} fusion(f32[8,2,18,18,130]{4,3,2,0,1:T(8,128)S(1)} %select_maximum_fusion.6), kind=kLoop, calls=%fused_computation.51 | loop fusion | flops 2621440 | bytes 14680064 | tf_op jit(solution)/shard_map/add | solution.py:17
  63.9 0.8 multiply_subtract_fusion.9
  64.7 2.4 select_maximum_fusion.5
  67.1 3.3 %slice_add_fusion.25 = f32[8,2,16,16,128]{4,3,2,0,1:T(8,128)S(1)} fusion(f32[8,2,18,18,130]{4,3,2,0,1:T(8,128)S(1)} %select_maximum_fusion.5), kind=kLoop, calls=%fused_computation.46 | loop fusion | flops 2621440 | bytes 14680064 | tf_op jit(solution)/shard_map/add | solution.py:17
  70.4 0.8 multiply_subtract_fusion.8
  71.2 2.4 select_maximum_fusion.4
  73.6 3.3 %slice_add_fusion.20 = f32[8,2,16,16,128]{4,3,2,0,1:T(8,128)S(1)} fusion(f32[8,2,18,18,130]{4,3,2,0,1:T(8,128)S(1)} %select_maximum_fusion.4), kind=kLoop, calls=%fused_computation.41 | loop fusion | flops 2621440 | bytes 14680064 | tf_op jit(solution)/shard_map/add | solution.py:17
  76.8 0.8 multiply_subtract_fusion.7
  77.6 2.6 select_maximum_fusion.3
  80.2 3.3 %slice_add_fusion.15 = f32[8,2,16,16,128]{4,3,2,0,1:T(8,128)S(1)} fusion(f32[8,2,18,18,130]{4,3,2,0,1:T(8,128)S(1)} %select_maximum_fusion.3), kind=kLoop, calls=%fused_computation.36 | loop fusion | flops 2621440 | bytes 14680064 | tf_op jit(solution)/shard_map/add | solution.py:17
  83.5 0.8 multiply_subtract_fusion.6
  84.3 2.4 select_maximum_fusion.2
  86.7 3.3 %slice_add_fusion.10 = f32[8,2,16,16,128]{4,3,2,0,1:T(8,128)S(1)} fusion(f32[8,2,18,18,130]{4,3,2,0,1:T(8,128)S(1)} %select_maximum_fusion.2), kind=kLoop, calls=%fused_computation.31 | loop fusion | flops 2621440 | bytes 14680064 | tf_op jit(solution)/shard_map/add | solution.py:17
  90.0 0.8 multiply_subtract_fusion.5
  90.8 2.4 select_maximum_fusion.1
  93.1 3.3 %slice_add_fusion.5 = f32[8,2,16,16,128]{4,3,2,0,1:T(8,128)S(1)} fusion(f32[8,2,18,18,130]{4,3,2,0,1:T(8,128)S(1)} %select_maximum_fusion.1), kind=kLoop, calls=%fused_computation.26 | loop fusion | flops 2621440 | bytes 14680064 | tf_op jit(solution)/shard_map/add | solution.py:17
  96.4 0.8 multiply_subtract_fusion.4
  97.2 2.4 select_maximum_fusion
  99.6 3.5 %slice_add_fusion = f32[8,2,16,16,128]{4,3,2,0,1:T(8,128)S(1)} fusion(f32[8,2,18,18,130]{4,3,2,0,1:T(8,128)S(1)} %select_maximum_fusion), kind=kLoop, calls=%fused_computation.21 | loop fusion | flops 2621440 | bytes 14680064 | tf_op jit(solution)/shard_map/add | solution.py:17
  103.1 0.9 multiply_subtract_fusion.1
  104.1 0.5 multiply_subtract_fusion
  104.6 0.4 maximum_bitcast_fusion
  105.0 0.4 pad_maximum_fusion
  105.4 0.6 copy.17
  106.0 51.6 %all_to_all.36 = f32[2,2,8,16,16,128]{5,4,2,1,0,3:T(8,128)S(1)} all-to-all(f32[2,2,8,16,16,128]{5,4,2,1,0,3:T(8,128)S(1)} %copy.17), channel_id=1, replica_groups=mesh['node'=4,'dom'=8] {'dom'}, dimensions={3} | all-to-all | bytes 8388608 | tf_op jit(solution)/shard_map/all_to_all | solution.py:84
  157.6 0.5 copy.19
  158.2 0.0 copy-start.1
  158.2 0.5 bitcast_reduce_fusion
  158.7 0.0 copy-start
  158.7 0.5 copy-done.1
  159.2 3.1 %fusion.10 = f32[2,2,32,32]{3,2,1,0:T(8,128)S(1)} fusion(f32[2,2,32,2,16,128]{5,4,3,2,1,0:T(8,128)S(1)} %bitcast_reduce_fusion, f32[32,2,16,128,1,1]{3,2,1,0,5,4:T(8,128)S(1)} %bitcast.53), kind=kOutput, calls=%fused_computation.66 | convolution fusion | flops 201330688 | bytes 2637824 | tf_op jit(solution)/shard_map/dot_general | solution.py:88
  162.3 0.0 all-reduce.10.cloned.1.call-start
  162.4 0.0 copy-done
  162.4 0.7 all-reduce.10.cloned.1.call-update
  163.1 42.9 %psum.15 = f32[2,2,32,32]{3,2,1,0:T(8,128)} all-reduce(f32[2,2,32,32]{3,2,1,0:T(8,128)S(1)} %fusion.10), channel_id=1, replica_groups=mesh['node'=4,'dom'=8] {'node','dom'}, use_global_device_ids=true, to_apply=%region_2.3 | all-reduce | flops 4096 | bytes 32768 | tf_op jit(solution)/shard_map/psum | solution.py:96
  206.0 46.1 %all-reduce.10.cloned.1.call-done = f32[2,2,32,2,16,128]{5,4,3,2,1,0:T(8,128)} async-done(((f32[2,2,32,2,16,128]{5,4,3,2,1,0:T(8,128)}), f32[2,2,32,2,16,128]{5,4,3,2,1,0:T(8,128)}) %all-reduce.10.cloned.1.call-update) | async-done | bytes 2097168 | tf_op jit(solution)/shard_map/psum | solution.py:97
  252.1 1.9 constant_dynamic-slice_fusion
  (1 shorter events, 0.0 us)
Async XLA Ops:
  7.2 7.4 %copy-start.2 = (f32[2,16,128]{2,1,0:T(8,128)S(1)}, f32[2,16,128]{2,1,0:T(8,128)}, u32[]{:S(2)}) copy-start(f32[2,16,128]{2,1,0:T(8,128)} %param.5) | copy-start | bytes 49156
  7.2 26.2 %copy-start.3 = (f32[2,16,128]{2,1,0:T(8,128)S(1)}, f32[2,16,128]{2,1,0:T(8,128)}, u32[]{:S(2)}) copy-start(f32[2,16,128]{2,1,0:T(8,128)} %param.6) | copy-start | bytes 49156
  7.2 34.5 %copy-start.4 = (f32[2,16,128]{2,1,0:T(8,128)S(1)}, f32[2,16,128]{2,1,0:T(8,128)}, u32[]{:S(2)}) copy-start(f32[2,16,128]{2,1,0:T(8,128)} %param.7) | copy-start | bytes 49156
  9.4 41.5 %all-to-all-start = ((f32[64,2,16,128]{3,2,1,0:T(8,128)}), f32[64,2,16,128]{3,2,1,0:T(8,128)S(1)}, u32[]{:S(2)}, u32[]{:S(2)}) async-start(f32[64,2,16,128]{3,2,1,0:T(8,128)} %bitcast), calls=%async_computation | async-start | bytes 2097152 | tf_op jit(solution)/shard_map/all_to_all | solution.py:58
  158.2 1.0 copy-start.1
  158.7 3.6 %copy-start = (f32[2,2,32,2,16,128]{5,4,3,2,1,0:T(8,128)}, f32[2,2,32,2,16,128]{5,4,3,2,1,0:T(8,128)S(1)}, u32[]{:S(2)}) copy-start(f32[2,2,32,2,16,128]{5,4,3,2,1,0:T(8,128)S(1)} %bitcast_reduce_fusion) | copy-start | bytes 6291460
  162.3 89.8 %all-reduce.10.cloned.1.call-start = ((), (), s32[]{:S(2)}) async-start(), calls=%async_computation.2 | async-start | bytes 4194304 | tf_op jit(solution)/shard_map/psum | solution.py:97
Sparse Core Ops, SparseCore 0:
  165.5 86.5 all-reduce.9
where the time goes:
time: 261 us
  blocking collectives  131 us (50%)
  other arithmetic  54.8 us (21%)
  waiting for transfers between devices  46.8 us (18%)
  between operations  14.3 us (5%)
  local copies, waits for them, and re-layouts  5.8 us (2%)
  starting transfers between devices  5.24 us (2%)
  matrix products  3.08 us (1%)
    all_to_all x1, blocking collectives, body(): back = lax.all_to_all(terms, 'dom', split_axis=3, concat_axis=2, tiled=True)  51.6 us
    psum x1, waiting for transfers between devices, body(): summed = lax.psum(local, 'node')  46.1 us
    psum x1, blocking collectives, body(): lax.psum(partial_value.reshape(2, 2, vectors, vectors) / cells, ('node',...  42.9 us
    add x8, other arithmetic, grid_step(): total = total + padded[:, :, 1:-1, 1:-1, 2:] + padded[:, :, 1:-1, 1:-1, :-2]  26.4 us
    all_gather x1, blocking collectives, body(): lax.all_gather(slope, 'dom', axis=0, tiled=True)  18.8 us
    another operation x7, other arithmetic, grid_step(): jnp.stack([real_part * factor_re - imag_part * factor_im, real_part * fac...  16.9 us
    all_gather x1, blocking collectives, body(): lax.all_gather(damping, 'dom', axis=0, tiled=True)  9.1 us
    all_gather x1, blocking collectives, body(): lax.all_gather(root, 'dom', axis=0, tiled=True)  8.31 us
  transfers between devices with their start and end apart: 2, of which 1 were waited for; matrix products, arithmetic and copies ran while one was open for 0% of the time, Pallas kernels for 0%

commit v1 on v0

--- a/solution.py
+++ b/solution.py
@@ -94,7 +94,10 @@
     )
     cells = planes * probes.shape[2] * probes.shape[3] * lax.axis_size("dom")
     projections = lax.psum(partial_value.reshape(2, 2, vectors, vectors) / cells, ("node", "dom"))
-    summed = lax.psum(local, "node")
+    size, summed = (lax.axis_size("node"), local)
+    for far in [1 << k for k in range(size.bit_length() - 1)]:
+        route = [(i, i ^ far) for i in range(size)]
+        summed = summed + lax.ppermute(summed, "node", route)
     share = vectors // groups
     moments = lax.dynamic_slice_in_dim(summed, lax.axis_index("node") * share, share, 2)
     return (moments, projections)

time: 261 us -> 318 us (1.22)
  blocking collectives: 131 us -> 196 us
  between operations: 14.3 us -> 0.93 us
  starting transfers between devices: 5.24 us -> 9.43 us
  other arithmetic: 54.8 us -> 58.8 us
    psum x1, blocking collectives: 42.9 us -> 108 us  [body(): lax.psum(partial_value.reshape(2, 2, vectors, vectors) / cells, ('node',...]
    psum x1 -> x0, waiting for transfers between devices: 46.1 us -> none  [body(): summed = lax.psum(local, 'node')]
    ppermute x0 -> x2, waiting for transfers between devices: none -> 45.2 us  [body(): summed = summed + lax.ppermute(summed, 'node', route)]
    ppermute x0 -> x2, starting transfers between devices: none -> 4.23 us  [body(): summed = summed + lax.ppermute(summed, 'node', route)]
    add x0 -> x2, other arithmetic: none -> 3.89 us  [body(): summed = summed + lax.ppermute(summed, 'node', route)]
  transfers between devices with their start and end apart: 2 -> 3, of which waited for: 1 -> 1; matrix products, arithmetic and copies ran while one was open for 0% -> 1% of each run, Pallas kernels for 0% -> 0%
where the time goes in v1:
time: 318 us; the launch traced here: 317 us
  blocking collectives  196 us (62%)
  other arithmetic  58.8 us (18%)
  waiting for transfers between devices  45.2 us (14%)
  starting transfers between devices  9.43 us (3%)
  local copies, waits for them, and re-layouts  3.41 us (1%)
    psum x1, blocking collectives, body(): lax.psum(partial_value.reshape(2, 2, vectors, vectors) / cells, ('node',...  108 us
    all_to_all x1, blocking collectives, body(): back = lax.all_to_all(terms, 'dom', split_axis=3, concat_axis=2, tiled=True)  51.6 us
    ppermute x2, waiting for transfers between devices, body(): summed = summed + lax.ppermute(summed, 'node', route)  45.2 us
    add x8, other arithmetic, grid_step(): total = total + padded[:, :, 1:-1, 1:-1, 2:] + padded[:, :, 1:-1, 1:-1, :-2]  26.4 us
    all_gather x1, blocking collectives, body(): lax.all_gather(slope, 'dom', axis=0, tiled=True)  18.8 us
    another operation x7, other arithmetic, grid_step(): jnp.stack([real_part * factor_re - imag_part * factor_im, real_part * fac...  16.9 us
    all_gather x1, blocking collectives, body(): lax.all_gather(damping, 'dom', axis=0, tiled=True)  9.1 us
    all_gather x1, blocking collectives, body(): lax.all_gather(root, 'dom', axis=0, tiled=True)  8.31 us
  transfers between devices with their start and end apart: 3, of which 1 were waited for; matrix products, arithmetic and copies ran while one was open for 1% of the time, Pallas kernels for 0%

profile of v1, /device:TPU:0, one launch (start us, length us, event | category | flops | bytes accessed | tf_op | source)
XLA Modules:
  0.0 317.1 jit_solution(12712035526979914572)
XLA Ops:
  0.6 0.0 copy-start.1
  0.6 0.0 copy-start.2
  0.7 0.0 copy-start.3
  0.7 2.2 broadcast_in_dim.2
  2.8 5.2 %all-to-all-start = ((f32[64,2,16,128]{3,2,1,0:T(8,128)}), f32[64,2,16,128]{3,2,1,0:T(8,128)S(1)}, u32[]{:S(2)}, u32[]{:S(2)}) async-start(f32[64,2,16,128]{3,2,1,0:T(8,128)} %bitcast), calls=%async_computation | async-start | bytes 2097152 | tf_op jit(solution)/shard_map/all_to_all | solution.py:58
  8.0 0.0 copy-done.1
  8.0 18.8 %all_gather.9 = f32[16,16,128]{2,1,0:T(8,128)S(1)} all-gather(f32[2,16,128]{2,1,0:T(8,128)S(1)} %copy-done.1), channel_id=1, replica_groups=mesh['node'=4,'dom'=8] {'dom'}, dimensions={0}, use_global_device_ids=true | all-gather | bytes 147456 | tf_op jit(solution)/shard_map/all_gather | solution.py:60
  26.9 0.0 copy-done.2
  26.9 8.3 %all_gather.10 = f32[16,16,128]{2,1,0:T(8,128)S(1)} all-gather(f32[2,16,128]{2,1,0:T(8,128)S(1)} %copy-done.2), channel_id=1, replica_groups=mesh['node'=4,'dom'=8] {'dom'}, dimensions={0}, use_global_device_ids=true | all-gather | bytes 147456 | tf_op jit(solution)/shard_map/all_gather | solution.py:61
  35.2 0.0 copy-done.3
  35.2 9.1 %all_gather.11 = f32[16,16,128]{2,1,0:T(8,128)S(1)} all-gather(f32[2,16,128]{2,1,0:T(8,128)S(1)} %copy-done.3), channel_id=1, replica_groups=mesh['node'=4,'dom'=8] {'dom'}, dimensions={0}, use_global_device_ids=true | all-gather | bytes 147456 | tf_op jit(solution)/shard_map/all_gather | solution.py:62
  44.3 0.1 multiply_subtract_fusion.12
  44.4 0.0 all-to-all-done
  44.4 0.1 copy.15
  44.5 0.6 fusion.19
  45.1 2.6 select_maximum_fusion.7
  47.7 3.3 %slice_add_fusion.35 = f32[8,2,16,16,128]{4,3,2,0,1:T(8,128)S(1)} fusion(f32[8,2,18,18,130]{4,3,2,0,1:T(8,128)S(1)} %select_maximum_fusion.7), kind=kLoop, calls=%fused_computation.56 | loop fusion | flops 2621440 | bytes 14680064 | tf_op jit(solution)/shard_map/add | solution.py:17
  50.9 0.8 multiply_subtract_fusion.10
  51.7 2.4 select_maximum_fusion.6
  54.1 3.3 %slice_add_fusion.30 = f32[8,2,16,16,128]{4,3,2,0,1:T(8,128)S(1)} fusion(f32[8,2,18,18,130]{4,3,2,0,1:T(8,128)S(1)} %select_maximum_fusion.6), kind=kLoop, calls=%fused_computation.51 | loop fusion | flops 2621440 | bytes 14680064 | tf_op jit(solution)/shard_map/add | solution.py:17
  57.4 0.8 multiply_subtract_fusion.9
  58.2 2.4 select_maximum_fusion.5
  60.6 3.3 %slice_add_fusion.25 = f32[8,2,16,16,128]{4,3,2,0,1:T(8,128)S(1)} fusion(f32[8,2,18,18,130]{4,3,2,0,1:T(8,128)S(1)} %select_maximum_fusion.5), kind=kLoop, calls=%fused_computation.46 | loop fusion | flops 2621440 | bytes 14680064 | tf_op jit(solution)/shard_map/add | solution.py:17
  63.8 0.8 multiply_subtract_fusion.8
  64.6 2.4 select_maximum_fusion.4
  67.0 3.3 %slice_add_fusion.20 = f32[8,2,16,16,128]{4,3,2,0,1:T(8,128)S(1)} fusion(f32[8,2,18,18,130]{4,3,2,0,1:T(8,128)S(1)} %select_maximum_fusion.4), kind=kLoop, calls=%fused_computation.41 | loop fusion | flops 2621440 | bytes 14680064 | tf_op jit(solution)/shard_map/add | solution.py:17
  70.3 0.8 multiply_subtract_fusion.7
  71.1 2.6 select_maximum_fusion.3
  73.7 3.3 %slice_add_fusion.15 = f32[8,2,16,16,128]{4,3,2,0,1:T(8,128)S(1)} fusion(f32[8,2,18,18,130]{4,3,2,0,1:T(8,128)S(1)} %select_maximum_fusion.3), kind=kLoop, calls=%fused_computation.36 | loop fusion | flops 2621440 | bytes 14680064 | tf_op jit(solution)/shard_map/add | solution.py:17
  77.0 0.8 multiply_subtract_fusion.6
  77.8 2.4 select_maximum_fusion.2
  80.1 3.3 %slice_add_fusion.10 = f32[8,2,16,16,128]{4,3,2,0,1:T(8,128)S(1)} fusion(f32[8,2,18,18,130]{4,3,2,0,1:T(8,128)S(1)} %select_maximum_fusion.2), kind=kLoop, calls=%fused_computation.31 | loop fusion | flops 2621440 | bytes 14680064 | tf_op jit(solution)/shard_map/add | solution.py:17
  83.4 0.8 multiply_subtract_fusion.5
  84.2 2.4 select_maximum_fusion.1
  86.6 3.3 %slice_add_fusion.5 = f32[8,2,16,16,128]{4,3,2,0,1:T(8,128)S(1)} fusion(f32[8,2,18,18,130]{4,3,2,0,1:T(8,128)S(1)} %select_maximum_fusion.1), kind=kLoop, calls=%fused_computation.26 | loop fusion | flops 2621440 | bytes 14680064 | tf_op jit(solution)/shard_map/add | solution.py:17
  89.9 0.8 multiply_subtract_fusion.4
  90.7 2.4 select_maximum_fusion
  93.0 3.5 %slice_add_fusion = f32[8,2,16,16,128]{4,3,2,0,1:T(8,128)S(1)} fusion(f32[8,2,18,18,130]{4,3,2,0,1:T(8,128)S(1)} %select_maximum_fusion), kind=kLoop, calls=%fused_computation.21 | loop fusion | flops 2621440 | bytes 14680064 | tf_op jit(solution)/shard_map/add | solution.py:17
  96.6 0.9 multiply_subtract_fusion.1
  97.5 0.5 multiply_subtract_fusion
  98.0 0.4 maximum_bitcast_fusion
  98.5 0.4 pad_maximum_fusion
  98.9 0.6 copy.17
  99.5 51.6 %all_to_all.36 = f32[2,2,8,16,16,128]{5,4,2,1,0,3:T(8,128)S(1)} all-to-all(f32[2,2,8,16,16,128]{5,4,2,1,0,3:T(8,128)S(1)} %copy.17), channel_id=1, replica_groups=mesh['node'=4,'dom'=8] {'dom'}, dimensions={3} | all-to-all | bytes 8388608 | tf_op jit(solution)/shard_map/all_to_all | solution.py:84
  151.1 0.5 copy.19
  151.7 0.5 bitcast_reduce_fusion
  152.2 0.0 copy-start
  152.2 1.6 collective-permute-start
  153.8 45.2 %collective-permute-done = f32[2,2,32,2,16,128]{5,4,3,2,1,0:T(8,128)S(1)} collective-permute-done((f32[2,2,32,2,16,128]{5,4,3,2,1,0:T(8,128)S(1)}, f32[2,2,32,2,16,128]{5,4,3,2,1,0:T(8,128)S(1)}, u32[]{:S(2)}, u32[]{:S(2)}) %collective-permute-start) | collective-permute-done | bytes 2097184 | tf_op jit(solution)/shard_map/ppermute | solution.py:100
  199.1 1.8 add.646
  200.9 2.6 collective-permute-start.1
  203.5 0.0 copy-done
  203.5 3.1 fusion.10
  206.6 108.5 %psum.7 = f32[2,2,32,32]{3,2,1,0:T(8,128)} all-reduce(f32[2,2,32,32]{3,2,1,0:T(8,128)S(1)} %fusion.10), channel_id=1, replica_groups=mesh['node'=4,'dom'=8] {'node','dom'}, use_global_device_ids=true, to_apply=%region_1.2 | all-reduce | flops 4096 | bytes 32768 | tf_op jit(solution)/shard_map/psum | solution.py:96
  315.1 0.0 collective-permute-done.1
  315.1 2.1 dynamic-slice_add_fusion
  (1 shorter events, 0.0 us)
Async XLA Ops:
  0.6 7.4 %copy-start.1 = (f32[2,16,128]{2,1,0:T(8,128)S(1)}, f32[2,16,128]{2,1,0:T(8,128)}, u32[]{:S(2)}) copy-start(f32[2,16,128]{2,1,0:T(8,128)} %param.5) | copy-start | bytes 49156
  0.6 26.2 %copy-start.2 = (f32[2,16,128]{2,1,0:T(8,128)S(1)}, f32[2,16,128]{2,1,0:T(8,128)}, u32[]{:S(2)}) copy-start(f32[2,16,128]{2,1,0:T(8,128)} %param.6) | copy-start | bytes 49156
  0.7 34.5 %copy-start.3 = (f32[2,16,128]{2,1,0:T(8,128)S(1)}, f32[2,16,128]{2,1,0:T(8,128)}, u32[]{:S(2)}) copy-start(f32[2,16,128]{2,1,0:T(8,128)} %param.7) | copy-start | bytes 49156
  2.8 41.5 %all-to-all-start = ((f32[64,2,16,128]{3,2,1,0:T(8,128)}), f32[64,2,16,128]{3,2,1,0:T(8,128)S(1)}, u32[]{:S(2)}, u32[]{:S(2)}) async-start(f32[64,2,16,128]{3,2,1,0:T(8,128)} %bitcast), calls=%async_computation | async-start | bytes 2097152 | tf_op jit(solution)/shard_map/all_to_all | solution.py:58
  152.2 51.3 %copy-start = (f32[32,2,16,128]{3,2,1,0:T(8,128)S(1)}, f32[32,2,16,128]{3,2,1,0:T(8,128)}, u32[]{:S(2)}) copy-start(f32[32,2,16,128]{3,2,1,0:T(8,128)} %param.4) | copy-start | bytes 1572868
  152.2 46.9 %collective-permute-start = (f32[2,2,32,2,16,128]{5,4,3,2,1,0:T(8,128)S(1)}, f32[2,2,32,2,16,128]{5,4,3,2,1,0:T(8,128)S(1)}, u32[]{:S(2)}, u32[]{:S(2)}) collective-permute-start(f32[2,2,32,2,16,128]{5,4,3,2,1,0:T(8,128)S(1)} %bitcast_reduce_fusion), channel_id=1, source_target_pairs={{0,8},{8,0},{16,24},{24,16},{1,9},{9,1},{17,25},{25,17},{2,10},{10... | collective-permute-start | bytes 6291464 | tf_op jit(solution)/shard_map/ppermute | solution.py:100
  200.9 114.2 %collective-permute-start.1 = (f32[2,2,32,2,16,128]{5,4,3,2,1,0:T(8,128)}, f32[2,2,32,2,16,128]{5,4,3,2,1,0:T(8,128)}, u32[]{:S(2)}, u32[]{:S(2)}) collective-permute-start(f32[2,2,32,2,16,128]{5,4,3,2,1,0:T(8,128)} %add.646), channel_id=1, source_target_pairs={{0,16},{8,24},{16,0},{24,8},{1,17},{9,25},{17,1},{25,9},{2,18},{10... | collective-permute-start | bytes 6291464 | tf_op jit(solution)/shard_map/ppermute | solution.py:100
